TPU v7x, 32 devices: a whole 2x2x4 slice. The times are simulated.
32 devices in a mesh: wave: 8 (over z, y), lev: 4 (over x, core).
Axes of the slice: x: 2, y: 2, z: 4, core: 2. Of those that a mesh axis runs over, the one named last changes fastest.
Arguments:
- spectral: float32 [8, 136, 2, 1280], P('wave', 'lev'), may hold values from -6 to 6
- to_modes: float32 [136, 136], replicated
- from_modes: float32 [136, 136], replicated
- mode_depths: float32 [136], replicated, may hold values from 0.05 to 5
- legendre: float32 [8, 16, 1280], P('wave'), may hold values from -0.03125 to 0.03125
- wave_ids: int32 [8], replicated, may hold values from 0 to 1279, as said below
- lat_points: int32 [16], P('wave'), may hold values from 20 to 5136, as said below
Outputs:
- grid: float32 [136, 16, 5136], P('lev', 'wave')
Inputs may be any that keep to these rules, and one draw needn't show every extreme that they name: `wave_ids`: distinct and ascending; 0 and 1279 are always among them. `lat_points`: each is 20 + 4 k for a whole k; not falling along the latitudes; the last is always 5136.
All inputs are finite; a program needn't handle non-finite values.
Results may differ from a plain program's by a relative error of at most 0.0003.
Values sent between devices are 32-bit elements; how exact they have to be, the bound alone decides.
No kernel may reach another device: no remote copies, remote signals or barrier semaphores. Data moves between devices by JAX's collectives and lax.ppermute only.
A program may use at most 64 MiB of HBM per device.

v0:
```python
import math
import jax
import jax.numpy as jnp
from jax import lax
from jax.sharding import PartitionSpec as P

LONS = 5136
two_pi = 2.0 * math.pi


def on_device(spectral, to_modes, from_modes, mode_depths, legendre, wave_ids, lat_points):
    highest = lax.Precision.HIGHEST
    waves_here = spectral.shape[0]
    total_orders = spectral.shape[3]
    block_len = total_orders // lax.axis_size("lev")
    columns = lax.all_to_all(spectral, "lev", split_axis=3, concat_axis=1, tiled=True)
    mode_coeffs = jnp.einsum("kl,wlcn->wkcn", to_modes, columns, precision=highest)
    first_order = lax.axis_index("lev") * block_len
    order_ids = first_order + jnp.arange(block_len)
    orders = order_ids.astype(jnp.float32)
    damping = 1.0 + mode_depths[:, None] * (orders * (orders + 1.0))[None, :] / float(
        total_orders * total_orders
    )
    divergence = jnp.einsum(
        "lk,wkcn->wlcn", from_modes, mode_coeffs / damping[None, :, None, :], precision=highest
    )
    own_ids = lax.dynamic_slice_in_dim(wave_ids, lax.axis_index("wave") * waves_here, waves_here)
    level_major = lax.all_to_all(divergence, "lev", split_axis=1, concat_axis=3, tiled=True)
    keep_mask = (jnp.arange(total_orders)[None, :] >= own_ids[:, None]).astype(jnp.float32)
    fourier = jnp.einsum(
        "wjn,wlcn->lwcj", legendre * keep_mask[:, None, :], level_major, precision=highest
    )
    band_data = lax.all_to_all(fourier, "wave", split_axis=3, concat_axis=1, tiled=True)
    positions = jnp.arange(LONS)

    def one_row(inputs):
        coeffs, points = inputs
        residue = wave_ids[:, None] * positions[None, :] % points
        phases = jnp.float32(two_pi) * residue.astype(jnp.float32) / points.astype(jnp.float32)
        weight = jnp.where(2 * wave_ids < points, jnp.where(wave_ids == 0, 1.0, 2.0), 0.0).astype(
            jnp.float32
        )
        basis_table = jnp.concatenate(
            [jnp.cos(phases) * weight[:, None], jnp.sin(phases) * weight[:, None]], 0
        )
        coefficient = jnp.concatenate([coeffs[:, :, 0], -coeffs[:, :, 1]], 1)
        lat_row = jnp.dot(coefficient, basis_table, precision=highest)
        return lat_row * (positions < points).astype(jnp.float32)[None, :]

    lat_rows = lax.map(one_row, (jnp.moveaxis(band_data, 3, 0), lat_points))
    return jnp.transpose(lat_rows, (1, 0, 2))


def solution(mesh):
    return jax.shard_map(
        on_device,
        mesh=mesh,
        in_specs=(
            P("wave", "lev", None, None),
            P(),
            P(),
            P(),
            P("wave", None, None),
            P(),
            P("wave"),
        ),
        out_specs=P("lev", "wave", None),
        check_vma=False,
    )
```

profile of v0, /device:TPU:0, one launch (start us, length us, event | category | flops | bytes accessed | tf_op | source)
XLA Modules:
  0.0 79.2 jit_solution(634367973494513038)
XLA Ops:
  0.0 2.6 %copy.29 = f32[1,34,2,1280]{1,2,0,3:T(2,128)S(1)} copy(f32[1,34,2,1280]{3,2,1,0:T(2,128)} %param.9) | data formatting | bytes 696320 | tf_op args[0]
  2.7 3.0 %reshape.90 = f32[4,1,21760]{2,1,0:T(1,128)} reshape(f32[1280,1,2,34]{3,2,1,0:T(2,128)S(1)} %bitcast.71) | data formatting | bytes 696320
  5.7 4.2 %all-to-all-start = ((f32[4,1,21760]{2,1,0:T(1,128)}), f32[4,1,21760]{2,1,0:T(1,128)S(1)}, u32[]{:S(2)}, u32[]{:S(2)}) async-start(f32[4,1,21760]{2,1,0:T(1,128)} %reshape.90), calls=%async_computation | async-start | bytes 696320 | tf_op jit(solution)/shard_map/all_to_all | solution.py:16
  10.0 6.9 %all-to-all-done = f32[4,1,21760]{2,1,0:T(1,128)S(1)} async-done(((f32[4,1,21760]{2,1,0:T(1,128)}), f32[4,1,21760]{2,1,0:T(1,128)S(1)}, u32[]{:S(2)}, u32[]{:S(2)}) %all-to-all-start) | async-done | bytes 348192 | tf_op jit(solution)/shard_map/all_to_all | solution.py:16
  17.4 1.6 %reduce = f32[4,21760]{1,0:T(4,128)S(1)} reduce(f32[4,1,21760]{2,1,0:T(1,128)S(1)} %all-to-all-done, f32[]{:T(128)} %broadcast.99), dimensions={1}, to_apply=%all_to_all.35.reduce_sub_computation | reduce | bytes 696324 | tf_op jit(solution)/shard_map/all_to_all | solution.py:16
  19.0 2.2 %reshape.91 = f32[1280,1,2,34]{3,2,1,0:T(2,128)S(1)} reshape(f32[4,21760]{1,0:T(4,128)S(1)} %reduce) | data formatting | bytes 696320
  21.3 1.3 %copy.30 = f32[1,34,2,4,320]{4,2,1,3,0:T(2,128)S(1)} copy(f32[1,34,2,4,320]{1,2,4,3,0:T(2,128)S(1)} %bitcast.70) | data formatting | bytes 696320 | tf_op jit(solution)/shard_map/all_to_all | solution.py:16
  23.6 1.0 %copy.32 = f32[1,136,2,320]{3,2,0,1:T(2,128)} copy(f32[1,136,2,320]{3,1,2,0:T(8,128)S(1)} %convolution_bitcast_fusion) | data formatting | bytes 696320 | tf_op jit(solution)/shard_map/lk,wkcn->wlcn/transpose | solution.py:24
  24.6 3.6 %all-to-all-start.1 = ((f32[1,136,2,320]{3,2,0,1:T(2,128)}), f32[1,136,2,320]{3,2,0,1:T(2,128)S(1)}, u32[]{:S(2)}, u32[]{:S(2)}) async-start(f32[1,136,2,320]{3,2,0,1:T(2,128)} %copy.32), calls=%async_computation.1 | async-start | bytes 835584 | tf_op jit(solution)/shard_map/all_to_all | solution.py:28
  28.2 0.7 dynamic_slice.11
  28.9 0.6 fusion.28
  29.5 6.4 %all-to-all-done.1 = f32[1,136,2,320]{3,2,0,1:T(2,128)S(1)} async-done(((f32[1,136,2,320]{3,2,0,1:T(2,128)}), f32[1,136,2,320]{3,2,0,1:T(2,128)S(1)}, u32[]{:S(2)}, u32[]{:S(2)}) %all-to-all-start.1) | async-done | bytes 348192 | tf_op jit(solution)/shard_map/all_to_all | solution.py:28
  36.3 0.8 convolution_bitcast_fusion.2
  37.1 0.7 reshape.92
  37.8 6.5 %all-to-all-start.2 = ((f32[8,1,136]{2,1,0:T(1,128)}), f32[8,1,136]{2,1,0:T(1,128)S(1)}, u32[]{:S(2)}, u32[]{:S(2)}) async-start(f32[8,1,136]{2,1,0:T(1,128)} %reshape.92), calls=%async_computation.2 | async-start | bytes 16384 | tf_op jit(solution)/shard_map/all_to_all | solution.py:33
  44.3 6.5 %all-to-all-done.2 = f32[8,1,136]{2,1,0:T(1,128)S(1)} async-done(((f32[8,1,136]{2,1,0:T(1,128)}), f32[8,1,136]{2,1,0:T(1,128)S(1)}, u32[]{:S(2)}, u32[]{:S(2)}) %all-to-all-start.2) | async-done | bytes 4384 | tf_op jit(solution)/shard_map/all_to_all | solution.py:33
  50.8 0.7 reduce.1
  51.6 26.6 %while.12 = (s32[]{:T(128)}, f32[2,34,5136]{2,0,1:T(2,128)S(1)}, f32[2,34,8,2]{1,2,3,0:T(8,128)S(1)}, s32[8]{0:T(128)S(1)}, s32[2]{0:T(128)S(1)}, /*index=5*/s32[]{:T(128)}, s32[]{:T(128)}) while((s32[]{:T(128)}, f32[2,34,5136]{2,0,1:T(2,128)S(1)}, f32[2,34,8,2]{1,2,3,0:T(8,128)S(1)}, s32[8]{0:T(128)S(1)}, ...), condition=%wide.region_1.2_spmd.clone.clone, body=%wide.region_0.1_spmd.clone.clone.sunk | while | flops 34329884 | bytes 4202137 | solution.py:50
  51.6 0.6 dynamic_slice.20
  53.5 0.6 compare_select_fusion.3
  54.8 2.3 %cosine_multiply_fusion.2 = (f32[8,5136]{1,0:T(8,128)S(1)}, f32[8,5136]{1,0:T(8,128)S(1)}) fusion(f32[8]{0:T(128)S(1)} %compare_select_fusion.3, f32[]{:T(128)S(6)} %convert_element_type.54, pred[]{:T(512)S(6)} %lt.78, s32[]{:T(128)S(6)} %select_n.59, s32[8]{0:T(128)S(1)} %get-tuple-element.139), kind=kLoop, calls=%fused_computation.15.clone.1 | loop fusion | flops 534144 | bytes 328777 | tf_op jit(solution)/shard_map/while/body/eval_jaxpr/mul | solution.py:44
  57.1 0.7 fusion.37
  57.8 0.9 %fusion.38 = f32[1,34,5136]{2,1,0:T(8,128)S(1)} fusion(f32[5136]{0:T(1024)S(1)} %fusion.37, f32[8,5136]{1,0:T(8,128)S(1)} %get-tuple-element.118, f32[8,5136]{1,0:T(8,128)S(1)} %get-tuple-element.119, f32[34,8]{0,1:T(8,128)S(1)} %get-tuple-element.120, f32[34,8]{0,1:T(8,128)S(1)} %get-tuple-element.121), kind=kOutput, calls=%fused_computation.2.clone.1 | convolution fusion | flops 33785152 | bytes 1049920 | tf_op jit(solution)/shard_map/while/body/eval_jaxpr/dot_general | solution.py:47
  58.7 0.7 copy.49
  59.4 5.3 %dynamic_update_slice.7 = f32[2,34,5136]{2,0,1:T(2,128)S(1)} dynamic-update-slice(f32[2,34,5136]{2,0,1:T(2,128)S(1)} %get-tuple-element.130, f32[1,34,5136]{2,0,1:T(1,128)S(1)} %copy.49, s32[]{:T(128)} %get-tuple-element.129, s32[]{:T(128)} %constant.25.clone.1..sunk, s32[]{:T(128)} %constant.25.clone.1..sunk) | dynamic-update-slice | bytes 1396996 | tf_op jit(solution)/shard_map/while/body/jit(dynamic_update_index_in_dim)/dynamic_update_slice | solution.py:50
  66.7 0.6 compare_select_fusion.3
  68.0 2.3 %cosine_multiply_fusion.2 = (f32[8,5136]{1,0:T(8,128)S(1)}, f32[8,5136]{1,0:T(8,128)S(1)}) fusion(f32[8]{0:T(128)S(1)} %compare_select_fusion.3, f32[]{:T(128)S(6)} %convert_element_type.54, pred[]{:T(512)S(6)} %lt.78, s32[]{:T(128)S(6)} %select_n.59, s32[8]{0:T(128)S(1)} %get-tuple-element.139), kind=kLoop, calls=%fused_computation.15.clone.1 | loop fusion | flops 534144 | bytes 328777 | tf_op jit(solution)/shard_map/while/body/eval_jaxpr/mul | solution.py:44
  70.3 0.7 fusion.37
  71.0 0.9 %fusion.38 = f32[1,34,5136]{2,1,0:T(8,128)S(1)} fusion(f32[5136]{0:T(1024)S(1)} %fusion.37, f32[8,5136]{1,0:T(8,128)S(1)} %get-tuple-element.118, f32[8,5136]{1,0:T(8,128)S(1)} %get-tuple-element.119, f32[34,8]{0,1:T(8,128)S(1)} %get-tuple-element.120, f32[34,8]{0,1:T(8,128)S(1)} %get-tuple-element.121), kind=kOutput, calls=%fused_computation.2.clone.1 | convolution fusion | flops 33785152 | bytes 1049920 | tf_op jit(solution)/shard_map/while/body/eval_jaxpr/dot_general | solution.py:47
  71.9 0.7 copy.49
  72.6 5.5 %dynamic_update_slice.7 = f32[2,34,5136]{2,0,1:T(2,128)S(1)} dynamic-update-slice(f32[2,34,5136]{2,0,1:T(2,128)S(1)} %get-tuple-element.130, f32[1,34,5136]{2,0,1:T(1,128)S(1)} %copy.49, s32[]{:T(128)} %get-tuple-element.129, s32[]{:T(128)} %constant.25.clone.1..sunk, s32[]{:T(128)} %constant.25.clone.1..sunk) | dynamic-update-slice | bytes 1396996 | tf_op jit(solution)/shard_map/while/body/jit(dynamic_update_index_in_dim)/dynamic_update_slice | solution.py:50
  78.1 1.1 %copy-done.5 = f32[2,34,5136]{2,0,1:T(2,128)} copy-done((f32[2,34,5136]{2,0,1:T(2,128)}, f32[2,34,5136]{2,0,1:T(2,128)S(1)}, u32[]{:S(2)}) %copy-start.5) | copy-done | bytes 1397016
  (29 shorter events, 2.8 us)
Async XLA Ops:
  0.0 22.5 %copy-start = (f32[136,136]{1,0:T(8,128)S(1)}, f32[136,136]{1,0:T(8,128)}, u32[]{:S(2)}) copy-start(f32[136,136]{1,0:T(8,128)} %param.10) | copy-start | bytes 221956
  2.6 7.3 %copy-start.4 = (f32[136]{0:T(256)S(1)}, f32[136]{0:T(256)}, u32[]{:S(2)}) copy-start(f32[136]{0:T(256)} %param.12) | copy-start | bytes 1636
  5.7 11.2 %all-to-all-start = ((f32[4,1,21760]{2,1,0:T(1,128)}), f32[4,1,21760]{2,1,0:T(1,128)S(1)}, u32[]{:S(2)}, u32[]{:S(2)}) async-start(f32[4,1,21760]{2,1,0:T(1,128)} %reshape.90), calls=%async_computation | async-start | bytes 696320 | tf_op jit(solution)/shard_map/all_to_all | solution.py:16
  21.3 1.8 %copy-start.1 = (f32[136,136]{1,0:T(8,128)S(1)}, f32[136,136]{1,0:T(8,128)}, u32[]{:S(2)}) copy-start(f32[136,136]{1,0:T(8,128)} %param.11) | copy-start | bytes 221956
  23.1 5.1 %copy-start.3 = (s32[8]{0:T(128)S(1)}, s32[8]{0:T(128)}, u32[]{:S(2)}) copy-start(s32[8]{0:T(128)} %param.14) | copy-start | bytes 100
  24.6 11.7 %copy-start.2 = (f32[1,16,1280]{2,1,0:T(8,128)S(1)}, f32[1,16,1280]{2,1,0:T(8,128)}, u32[]{:S(2)}) copy-start(f32[1,16,1280]{2,1,0:T(8,128)} %param.13) | copy-start | bytes 245764
  24.6 27.0 %copy-start.6 = (s32[2]{0:T(128)S(1)}, s32[2]{0:T(128)}, u32[]{:S(2)}) copy-start(s32[2]{0:T(128)} %param.15) | copy-start | bytes 28
  24.6 11.3 %all-to-all-start.1 = ((f32[1,136,2,320]{3,2,0,1:T(2,128)}), f32[1,136,2,320]{3,2,0,1:T(2,128)S(1)}, u32[]{:S(2)}, u32[]{:S(2)}) async-start(f32[1,136,2,320]{3,2,0,1:T(2,128)} %copy.32), calls=%async_computation.1 | async-start | bytes 835584 | tf_op jit(solution)/shard_map/all_to_all | solution.py:28
  37.8 13.0 %all-to-all-start.2 = ((f32[8,1,136]{2,1,0:T(1,128)}), f32[8,1,136]{2,1,0:T(1,128)S(1)}, u32[]{:S(2)}, u32[]{:S(2)}) async-start(f32[8,1,136]{2,1,0:T(1,128)} %reshape.92), calls=%async_computation.2 | async-start | bytes 16384 | tf_op jit(solution)/shard_map/all_to_all | solution.py:33
  78.1 1.1 %copy-start.5 = (f32[2,34,5136]{2,0,1:T(2,128)}, f32[2,34,5136]{2,0,1:T(2,128)S(1)}, u32[]{:S(2)}) copy-start(f32[2,34,5136]{2,0,1:T(2,128)S(1)} %get-tuple-element.40) | copy-start | bytes 4190980
where the time goes:
time: 79.7 us; the launch traced here: 79.2 us
  local copies, waits for them, and re-layouts  27.1 us (34%)
  waiting for transfers between devices  19.7 us (25%)
  starting transfers between devices  14.3 us (18%)
  other arithmetic  10.3 us (13%)
  loops' own time  4.04 us (5%)
  matrix products  3.55 us (4%)
    dynamic_update_slice x4, local copies, waits for them, and re-layouts, on_device(): lat_rows = lax.map(one_row, (jnp.moveaxis(band_data, 3, 0), lat_points))  12.3 us
    unnamed x19, local copies, waits for them, and re-layouts  9.8 us
    all_to_all x1, waiting for transfers between devices, on_device(): lax.all_to_all(spectral, 'lev', split_axis=3, concat_axis=1, tiled=True)  6.85 us
    all_to_all x1, waiting for transfers between devices, on_device(): lax.all_to_all(fourier, 'wave', split_axis=3, concat_axis=1, tiled=True)  6.51 us
    all_to_all x1, starting transfers between devices, on_device(): lax.all_to_all(fourier, 'wave', split_axis=3, concat_axis=1, tiled=True)  6.5 us
    all_to_all x1, waiting for transfers between devices, on_device(): lax.all_to_all(divergence, 'lev', split_axis=1, concat_axis=3, tiled=True)  6.37 us
    mul x2, other arithmetic, one_row(): jnp.cos(phases) * weight[:, None]  4.69 us
    all_to_all x1, starting transfers between devices, on_device(): lax.all_to_all(spectral, 'lev', split_axis=3, concat_axis=1, tiled=True)  4.21 us
  transfers between devices with their start and end apart: 3, of which 3 were waited for; matrix products, arithmetic and copies ran while one was open for 2% of the time, Pallas kernels for 0%

commit v1 on v0

--- a/solution.py
+++ b/solution.py
@@ -6,6 +6,29 @@
 
 LONS = 5136
 two_pi = 2.0 * math.pi
+
+
+def split_up(x, dim, devices):
+    dims = x.shape
+    blocks = x.reshape(*dims[:dim], devices, dims[dim] // devices, *dims[dim + 1 :])
+    return jnp.moveaxis(blocks, dim, 0)
+
+
+def joined_along(pieces, dim):
+    shape = list(pieces.shape[1:])
+    shape[dim] *= pieces.shape[0]
+    return jnp.moveaxis(pieces, 0, dim).reshape(shape)
+
+
+def exchange_in_pairs(value, axis, split_dim, concat_dim):
+    size, index = (lax.axis_size(axis), lax.axis_index(axis))
+    blocks = split_up(value, split_dim, size)
+    gathered = [blocks[index]]
+    for turn in range(1, size):
+        sent = blocks[index ^ turn]
+        gathered.append(lax.ppermute(sent, axis, [(i, i ^ turn) for i in range(size)]))
+    blocks = jnp.stack(gathered)[index ^ jnp.arange(size)]
+    return joined_along(blocks, concat_dim)
 
 
 def on_device(spectral, to_modes, from_modes, mode_depths, legendre, wave_ids, lat_points):
@@ -30,7 +53,7 @@
     fourier = jnp.einsum(
         "wjn,wlcn->lwcj", legendre * keep_mask[:, None, :], level_major, precision=highest
     )
-    band_data = lax.all_to_all(fourier, "wave", split_axis=3, concat_axis=1, tiled=True)
+    band_data = exchange_in_pairs(fourier, "wave", 3, 1)
     positions = jnp.arange(LONS)
 
     def one_row(inputs):

time: 79.7 us -> 84 us (1.054)
  starting transfers between devices: 14.3 us -> 19.6 us
    ppermute x0 -> x7, starting transfers between devices: none -> 11.7 us  [exchange_in_pairs(): lax.ppermute(sent, axis, [(i, i ^ turn) for i in range(size)])]
    all_to_all x1 -> x0, waiting for transfers between devices: 6.51 us -> none  [on_device(): lax.all_to_all(fourier, 'wave', split_axis=3, concat_axis=1, tiled=True)]
    all_to_all x1 -> x0, starting transfers between devices: 6.5 us -> none  [on_device(): lax.all_to_all(fourier, 'wave', split_axis=3, concat_axis=1, tiled=True)]
    ppermute x0 -> x7, waiting for transfers between devices: none -> 6.21 us  [exchange_in_pairs(): lax.ppermute(sent, axis, [(i, i ^ turn) for i in range(size)])]
    all_to_all x1, waiting for transfers between devices: 6.85 us -> 5.47 us  [on_device(): lax.all_to_all(spectral, 'lev', split_axis=3, concat_axis=1, tiled=True)]
    all_to_all x1, waiting for transfers between devices: 6.37 us -> 7.29 us  [on_device(): lax.all_to_all(divergence, 'lev', split_axis=1, concat_axis=3, tiled=True)]
    unnamed x19 -> x24, local copies, waits for them, and re-layouts: 9.8 us -> 9.07 us
  transfers between devices with their start and end apart: 3 -> 9, of which waited for: 3 -> 5; matrix products, arithmetic and copies ran while one was open for 2% -> 2% of each run, Pallas kernels for 0% -> 0%
where the time goes in v1:
time: 84 us; the launch traced here: 83.6 us
  local copies, waits for them, and re-layouts  27.4 us (33%)
  starting transfers between devices  19.6 us (23%)
  waiting for transfers between devices  19 us (23%)
  other arithmetic  9.74 us (12%)
  loops' own time  4.05 us (5%)
  matrix products  3.57 us (4%)
    dynamic_update_slice x4, local copies, waits for them, and re-layouts, on_device(): lat_rows = lax.map(one_row, (jnp.moveaxis(band_data, 3, 0), lat_points))  12.6 us
    ppermute x7, starting transfers between devices, exchange_in_pairs(): lax.ppermute(sent, axis, [(i, i ^ turn) for i in range(size)])  11.7 us
    unnamed x24, local copies, waits for them, and re-layouts  9.07 us
    all_to_all x1, waiting for transfers between devices, on_device(): lax.all_to_all(divergence, 'lev', split_axis=1, concat_axis=3, tiled=True)  7.29 us
    ppermute x7, waiting for transfers between devices, exchange_in_pairs(): lax.ppermute(sent, axis, [(i, i ^ turn) for i in range(size)])  6.21 us
    all_to_all x1, waiting for transfers between devices, on_device(): lax.all_to_all(spectral, 'lev', split_axis=3, concat_axis=1, tiled=True)  5.47 us
    mul x2, other arithmetic, one_row(): jnp.cos(phases) * weight[:, None]  4.69 us
    all_to_all x1, starting transfers between devices, on_device(): lax.all_to_all(spectral, 'lev', split_axis=3, concat_axis=1, tiled=True)  4.21 us
  transfers between devices with their start and end apart: 9, of which 5 were waited for; matrix products, arithmetic and copies ran while one was open for 2% of the time, Pallas kernels for 0%

profile of v1, /device:TPU:0, one launch (start us, length us, event | category | flops | bytes accessed | tf_op | source)
XLA Modules:
  0.0 83.6 jit_solution(6327551534290097055)
XLA Ops:
  0.0 2.6 %copy.30 = f32[1,34,2,1280]{1,2,0,3:T(2,128)S(1)} copy(f32[1,34,2,1280]{3,2,1,0:T(2,128)} %param.9) | data formatting | bytes 696320 | tf_op args[0]
  2.7 3.0 %reshape.157 = f32[4,1,21760]{2,1,0:T(1,128)} reshape(f32[1280,1,2,34]{3,2,1,0:T(2,128)S(1)} %bitcast.92) | data formatting | bytes 696320
  5.7 4.2 %all-to-all-start = ((f32[4,1,21760]{2,1,0:T(1,128)}), f32[4,1,21760]{2,1,0:T(1,128)S(1)}, u32[]{:S(2)}, u32[]{:S(2)}) async-start(f32[4,1,21760]{2,1,0:T(1,128)} %reshape.157), calls=%async_computation | async-start | bytes 696320 | tf_op jit(solution)/shard_map/all_to_all | solution.py:39
  9.9 0.7 dynamic_slice.11
  10.6 0.7 fusion.29
  11.4 5.5 %all-to-all-done = f32[4,1,21760]{2,1,0:T(1,128)S(1)} async-done(((f32[4,1,21760]{2,1,0:T(1,128)}), f32[4,1,21760]{2,1,0:T(1,128)S(1)}, u32[]{:S(2)}, u32[]{:S(2)}) %all-to-all-start) | async-done | bytes 348192 | tf_op jit(solution)/shard_map/all_to_all | solution.py:39
  17.4 1.6 %reduce = f32[4,21760]{1,0:T(4,128)S(1)} reduce(f32[4,1,21760]{2,1,0:T(1,128)S(1)} %all-to-all-done, f32[]{:T(128)} %broadcast.134), dimensions={1}, to_apply=%all_to_all.22.reduce_sub_computation | reduce | bytes 696324 | tf_op jit(solution)/shard_map/all_to_all | solution.py:39
  19.0 2.2 %reshape.158 = f32[1280,1,2,34]{3,2,1,0:T(2,128)S(1)} reshape(f32[4,21760]{1,0:T(4,128)S(1)} %reduce) | data formatting | bytes 696320
  21.3 1.3 %copy.31 = f32[1,34,2,4,320]{4,2,1,3,0:T(2,128)S(1)} copy(f32[1,34,2,4,320]{1,2,4,3,0:T(2,128)S(1)} %bitcast.91) | data formatting | bytes 696320 | tf_op jit(solution)/shard_map/all_to_all | solution.py:39
  23.6 1.0 %copy.33 = f32[1,136,2,320]{3,2,0,1:T(2,128)} copy(f32[1,136,2,320]{3,1,2,0:T(8,128)S(1)} %convolution_bitcast_fusion) | data formatting | bytes 696320 | tf_op jit(solution)/shard_map/lk,wkcn->wlcn/transpose | solution.py:47
  24.6 3.6 %all-to-all-start.1 = ((f32[1,136,2,320]{3,2,0,1:T(2,128)}), f32[1,136,2,320]{3,2,0,1:T(2,128)S(1)}, u32[]{:S(2)}, u32[]{:S(2)}) async-start(f32[1,136,2,320]{3,2,0,1:T(2,128)} %copy.33), calls=%async_computation.1 | async-start | bytes 835584 | tf_op jit(solution)/shard_map/all_to_all | solution.py:51
  28.4 7.3 %all-to-all-done.1 = f32[1,136,2,320]{3,2,0,1:T(2,128)S(1)} async-done(((f32[1,136,2,320]{3,2,0,1:T(2,128)}), f32[1,136,2,320]{3,2,0,1:T(2,128)S(1)}, u32[]{:S(2)}, u32[]{:S(2)}) %all-to-all-start.1) | async-done | bytes 348192 | tf_op jit(solution)/shard_map/all_to_all | solution.py:51
  36.1 0.8 fusion.23
  36.9 2.3 %collective-permute-start = (f32[34,1,2,2]{0,3,2,1:T(2,128)S(1)}, f32[34,1,2,2]{0,3,2,1:T(2,128)S(1)}, u32[]{:S(2)}, u32[]{:S(2)}) collective-permute-start(f32[34,1,2,2]{0,3,2,1:T(2,128)S(1)} %bitcast.104), channel_id=1, source_target_pairs={{0,4},{4,0},{8,12},{12,8},{16,20},{20,16},{24,28},{28,24},{1,5},{5... | collective-permute-start | bytes 1640 | tf_op jit(solution)/shard_map/ppermute | solution.py:29
  39.2 1.6 %collective-permute-start.1 = (f32[34,1,2,2]{0,3,2,1:T(2,128)S(1)}, f32[34,1,2,2]{0,3,2,1:T(2,128)S(1)}, u32[]{:S(2)}, u32[]{:S(2)}) collective-permute-start(f32[34,1,2,2]{0,3,2,1:T(2,128)S(1)} %bitcast.103), channel_id=1, source_target_pairs={{0,8},{4,12},{8,0},{12,4},{16,24},{20,28},{24,16},{28,20},{1,9},{5... | collective-permute-start | bytes 1640 | tf_op jit(solution)/shard_map/ppermute | solution.py:29
  40.8 3.0 %collective-permute-start.3 = (f32[34,1,2,2]{0,3,2,1:T(2,128)S(1)}, f32[34,1,2,2]{0,3,2,1:T(2,128)S(1)}, u32[]{:S(2)}, u32[]{:S(2)}) collective-permute-start(f32[34,1,2,2]{0,3,2,1:T(2,128)S(1)} %bitcast.101), channel_id=1, source_target_pairs={{0,16},{4,20},{8,24},{12,28},{16,0},{20,4},{24,8},{28,12},{1,17},{... | collective-permute-start | bytes 1640 | tf_op jit(solution)/shard_map/ppermute | solution.py:29
  43.8 1.3 %collective-permute-start.4 = (f32[34,1,2,2]{0,3,2,1:T(2,128)S(1)}, f32[34,1,2,2]{0,3,2,1:T(2,128)S(1)}, u32[]{:S(2)}, u32[]{:S(2)}) collective-permute-start(f32[34,1,2,2]{0,3,2,1:T(2,128)S(1)} %bitcast.100), channel_id=1, source_target_pairs={{0,20},{4,16},{8,28},{12,24},{16,4},{20,0},{24,12},{28,8},{1,21},{... | collective-permute-start | bytes 1640 | tf_op jit(solution)/shard_map/ppermute | solution.py:29
  45.1 3.6 %collective-permute-start.5 = (f32[34,1,2,2]{0,3,2,1:T(2,128)S(1)}, f32[34,1,2,2]{0,3,2,1:T(2,128)S(1)}, u32[]{:S(2)}, u32[]{:S(2)}) collective-permute-start(f32[34,1,2,2]{0,3,2,1:T(2,128)S(1)} %bitcast.99), channel_id=1, source_target_pairs={{0,24},{4,28},{8,16},{12,20},{16,8},{20,12},{24,0},{28,4},{1,25},{... | collective-permute-start | bytes 1640 | tf_op jit(solution)/shard_map/ppermute | solution.py:29
  49.2 1.3 %collective-permute-done.5 = f32[34,1,2,2]{0,3,2,1:T(2,128)S(1)} collective-permute-done((f32[34,1,2,2]{0,3,2,1:T(2,128)S(1)}, f32[34,1,2,2]{0,3,2,1:T(2,128)S(1)}, u32[]{:S(2)}, u32[]{:S(2)}) %collective-permute-start.5) | collective-permute-done | bytes 576 | tf_op jit(solution)/shard_map/ppermute | solution.py:29
  50.5 4.5 %collective-permute-done.6 = f32[34,1,2,2]{0,3,2,1:T(2,128)S(1)} collective-permute-done((f32[34,1,2,2]{0,3,2,1:T(2,128)S(1)}, f32[34,1,2,2]{0,3,2,1:T(2,128)S(1)}, u32[]{:S(2)}, u32[]{:S(2)}) %collective-permute-start.6) | collective-permute-done | bytes 576 | tf_op jit(solution)/shard_map/ppermute | solution.py:29
  55.5 26.9 %while.12 = (s32[]{:T(128)}, f32[2,34,5136]{2,0,1:T(2,128)S(1)}, f32[2,34,8,2]{1,0,3,2:T(2,128)S(1)}, s32[8]{0:T(128)S(1)}, s32[2]{0:T(128)S(1)}, /*index=5*/s32[]{:T(128)}, s32[]{:T(128)}) while((s32[]{:T(128)}, f32[2,34,5136]{2,0,1:T(2,128)S(1)}, f32[2,34,8,2]{1,0,3,2:T(2,128)S(1)}, s32[8]{0:T(128)S(1)}, ...), condition=%wide.region_1.2_spmd.clone.clone, body=%wide.region_0.1_spmd.clone.clone.sunk | while | flops 34329884 | bytes 4206489 | solution.py:73
  58.8 2.3 %cosine_multiply_fusion.2 = (f32[8,5136]{1,0:T(8,128)S(1)}, f32[8,5136]{1,0:T(8,128)S(1)}) fusion(f32[8]{0:T(128)S(1)} %compare_select_fusion.4, f32[]{:T(128)S(6)} %convert_element_type.54, pred[]{:T(512)S(6)} %lt.121, s32[]{:T(128)S(6)} %select_n.102, s32[8]{0:T(128)S(1)} %get-tuple-element.162), kind=kLoop, calls=%fused_computation.16.clone.1 | loop fusion | flops 534144 | bytes 328777 | tf_op jit(solution)/shard_map/while/body/eval_jaxpr/mul | solution.py:67
  61.1 0.7 fusion.38
  61.8 0.9 %fusion.39 = f32[1,34,5136]{2,1,0:T(8,128)S(1)} fusion(f32[5136]{0:T(1024)S(1)} %fusion.38, f32[8,5136]{1,0:T(8,128)S(1)} %get-tuple-element.141, f32[8,5136]{1,0:T(8,128)S(1)} %get-tuple-element.142, f32[34,8]{0,1:T(8,128)S(1)} %get-tuple-element.143, f32[34,8]{0,1:T(8,128)S(1)} %get-tuple-element.144), kind=kOutput, calls=%fused_computation.3.clone.1 | convolution fusion | flops 33785152 | bytes 1049920 | tf_op jit(solution)/shard_map/while/body/eval_jaxpr/dot_general | solution.py:70
  62.7 0.7 copy.56
  63.4 5.5 %dynamic_update_slice.7 = f32[2,34,5136]{2,0,1:T(2,128)S(1)} dynamic-update-slice(f32[2,34,5136]{2,0,1:T(2,128)S(1)} %get-tuple-element.153, f32[1,34,5136]{2,0,1:T(1,128)S(1)} %copy.56, s32[]{:T(128)} %get-tuple-element.152, s32[]{:T(128)} %constant.11.clone.1..sunk, s32[]{:T(128)} %constant.11.clone.1..sunk) | dynamic-update-slice | bytes 1396996 | tf_op jit(solution)/shard_map/while/body/jit(dynamic_update_index_in_dim)/dynamic_update_slice | solution.py:73
  72.1 2.3 %cosine_multiply_fusion.2 = (f32[8,5136]{1,0:T(8,128)S(1)}, f32[8,5136]{1,0:T(8,128)S(1)}) fusion(f32[8]{0:T(128)S(1)} %compare_select_fusion.4, f32[]{:T(128)S(6)} %convert_element_type.54, pred[]{:T(512)S(6)} %lt.121, s32[]{:T(128)S(6)} %select_n.102, s32[8]{0:T(128)S(1)} %get-tuple-element.162), kind=kLoop, calls=%fused_computation.16.clone.1 | loop fusion | flops 534144 | bytes 328777 | tf_op jit(solution)/shard_map/while/body/eval_jaxpr/mul | solution.py:67
  74.5 0.7 fusion.38
  75.2 0.9 %fusion.39 = f32[1,34,5136]{2,1,0:T(8,128)S(1)} fusion(f32[5136]{0:T(1024)S(1)} %fusion.38, f32[8,5136]{1,0:T(8,128)S(1)} %get-tuple-element.141, f32[8,5136]{1,0:T(8,128)S(1)} %get-tuple-element.142, f32[34,8]{0,1:T(8,128)S(1)} %get-tuple-element.143, f32[34,8]{0,1:T(8,128)S(1)} %get-tuple-element.144), kind=kOutput, calls=%fused_computation.3.clone.1 | convolution fusion | flops 33785152 | bytes 1049920 | tf_op jit(solution)/shard_map/while/body/eval_jaxpr/dot_general | solution.py:70
  76.1 0.7 copy.56
  76.8 5.7 %dynamic_update_slice.7 = f32[2,34,5136]{2,0,1:T(2,128)S(1)} dynamic-update-slice(f32[2,34,5136]{2,0,1:T(2,128)S(1)} %get-tuple-element.153, f32[1,34,5136]{2,0,1:T(1,128)S(1)} %copy.56, s32[]{:T(128)} %get-tuple-element.152, s32[]{:T(128)} %constant.11.clone.1..sunk, s32[]{:T(128)} %constant.11.clone.1..sunk) | dynamic-update-slice | bytes 1396996 | tf_op jit(solution)/shard_map/while/body/jit(dynamic_update_index_in_dim)/dynamic_update_slice | solution.py:73
  82.5 1.1 %copy-done.5 = f32[2,34,5136]{2,0,1:T(2,128)} copy-done((f32[2,34,5136]{2,0,1:T(2,128)}, f32[2,34,5136]{2,0,1:T(2,128)S(1)}, u32[]{:S(2)}) %copy-start.5) | copy-done | bytes 1397016
  (52 shorter events, 5.8 us)
Async XLA Ops:
  0.0 22.5 %copy-start = (f32[136,136]{1,0:T(8,128)S(1)}, f32[136,136]{1,0:T(8,128)}, u32[]{:S(2)}) copy-start(f32[136,136]{1,0:T(8,128)} %param.10) | copy-start | bytes 221956
  2.6 7.3 %copy-start.3 = (s32[8]{0:T(128)S(1)}, s32[8]{0:T(128)}, u32[]{:S(2)}) copy-start(s32[8]{0:T(128)} %param.14) | copy-start | bytes 100
  2.7 8.6 %copy-start.4 = (f32[136]{0:T(256)S(1)}, f32[136]{0:T(256)}, u32[]{:S(2)}) copy-start(f32[136]{0:T(256)} %param.12) | copy-start | bytes 1636
  5.7 11.2 %all-to-all-start = ((f32[4,1,21760]{2,1,0:T(1,128)}), f32[4,1,21760]{2,1,0:T(1,128)S(1)}, u32[]{:S(2)}, u32[]{:S(2)}) async-start(f32[4,1,21760]{2,1,0:T(1,128)} %reshape.157), calls=%async_computation | async-start | bytes 696320 | tf_op jit(solution)/shard_map/all_to_all | solution.py:39
  21.2 1.8 %copy-start.1 = (f32[136,136]{1,0:T(8,128)S(1)}, f32[136,136]{1,0:T(8,128)}, u32[]{:S(2)}) copy-start(f32[136,136]{1,0:T(8,128)} %param.11) | copy-start | bytes 221956
  23.1 5.2 %copy-start.2 = (f32[1,16,1280]{2,1,0:T(8,128)S(1)}, f32[1,16,1280]{2,1,0:T(8,128)}, u32[]{:S(2)}) copy-start(f32[1,16,1280]{2,1,0:T(8,128)} %param.13) | copy-start | bytes 245764
  24.6 11.1 %all-to-all-start.1 = ((f32[1,136,2,320]{3,2,0,1:T(2,128)}), f32[1,136,2,320]{3,2,0,1:T(2,128)S(1)}, u32[]{:S(2)}, u32[]{:S(2)}) async-start(f32[1,136,2,320]{3,2,0,1:T(2,128)} %copy.33), calls=%async_computation.1 | async-start | bytes 835584 | tf_op jit(solution)/shard_map/all_to_all | solution.py:51
  28.4 27.2 %copy-start.6 = (s32[2]{0:T(128)S(1)}, s32[2]{0:T(128)}, u32[]{:S(2)}) copy-start(s32[2]{0:T(128)} %param.15) | copy-start | bytes 28
  36.9 8.1 %collective-permute-start = (f32[34,1,2,2]{0,3,2,1:T(2,128)S(1)}, f32[34,1,2,2]{0,3,2,1:T(2,128)S(1)}, u32[]{:S(2)}, u32[]{:S(2)}) collective-permute-start(f32[34,1,2,2]{0,3,2,1:T(2,128)S(1)} %bitcast.104), channel_id=1, source_target_pairs={{0,4},{4,0},{8,12},{12,8},{16,20},{20,16},{24,28},{28,24},{1,5},{5... | collective-permute-start | bytes 1640 | tf_op jit(solution)/shard_map/ppermute | solution.py:29
  39.2 9.5 %collective-permute-start.1 = (f32[34,1,2,2]{0,3,2,1:T(2,128)S(1)}, f32[34,1,2,2]{0,3,2,1:T(2,128)S(1)}, u32[]{:S(2)}, u32[]{:S(2)}) collective-permute-start(f32[34,1,2,2]{0,3,2,1:T(2,128)S(1)} %bitcast.103), channel_id=1, source_target_pairs={{0,8},{4,12},{8,0},{12,4},{16,24},{20,28},{24,16},{28,20},{1,9},{5... | collective-permute-start | bytes 1640 | tf_op jit(solution)/shard_map/ppermute | solution.py:29
  40.8 7.9 %collective-permute-start.2 = (f32[34,1,2,2]{0,3,2,1:T(2,128)S(1)}, f32[34,1,2,2]{0,3,2,1:T(2,128)S(1)}, u32[]{:S(2)}, u32[]{:S(2)}) collective-permute-start(f32[34,1,2,2]{0,3,2,1:T(2,128)S(1)} %bitcast.102), channel_id=1, source_target_pairs={{0,12},{4,8},{8,4},{12,0},{16,28},{20,24},{24,20},{28,16},{1,13},{... | collective-permute-start | bytes 1640 | tf_op jit(solution)/shard_map/ppermute | solution.py:29
  40.8 7.9 %collective-permute-start.3 = (f32[34,1,2,2]{0,3,2,1:T(2,128)S(1)}, f32[34,1,2,2]{0,3,2,1:T(2,128)S(1)}, u32[]{:S(2)}, u32[]{:S(2)}) collective-permute-start(f32[34,1,2,2]{0,3,2,1:T(2,128)S(1)} %bitcast.101), channel_id=1, source_target_pairs={{0,16},{4,20},{8,24},{12,28},{16,0},{20,4},{24,8},{28,12},{1,17},{... | collective-permute-start | bytes 1640 | tf_op jit(solution)/shard_map/ppermute | solution.py:29
  43.8 5.4 %collective-permute-start.4 = (f32[34,1,2,2]{0,3,2,1:T(2,128)S(1)}, f32[34,1,2,2]{0,3,2,1:T(2,128)S(1)}, u32[]{:S(2)}, u32[]{:S(2)}) collective-permute-start(f32[34,1,2,2]{0,3,2,1:T(2,128)S(1)} %bitcast.100), channel_id=1, source_target_pairs={{0,20},{4,16},{8,28},{12,24},{16,4},{20,0},{24,12},{28,8},{1,21},{... | collective-permute-start | bytes 1640 | tf_op jit(solution)/shard_map/ppermute | solution.py:29
  45.1 5.4 %collective-permute-start.5 = (f32[34,1,2,2]{0,3,2,1:T(2,128)S(1)}, f32[34,1,2,2]{0,3,2,1:T(2,128)S(1)}, u32[]{:S(2)}, u32[]{:S(2)}) collective-permute-start(f32[34,1,2,2]{0,3,2,1:T(2,128)S(1)} %bitcast.99), channel_id=1, source_target_pairs={{0,24},{4,28},{8,16},{12,20},{16,8},{20,12},{24,0},{28,4},{1,25},{... | collective-permute-start | bytes 1640 | tf_op jit(solution)/shard_map/ppermute | solution.py:29
  48.7 6.3 %collective-permute-start.6 = (f32[34,1,2,2]{0,3,2,1:T(2,128)S(1)}, f32[34,1,2,2]{0,3,2,1:T(2,128)S(1)}, u32[]{:S(2)}, u32[]{:S(2)}) collective-permute-start(f32[34,1,2,2]{0,3,2,1:T(2,128)S(1)} %bitcast.98), channel_id=1, source_target_pairs={{0,28},{4,24},{8,20},{12,16},{16,12},{20,8},{24,4},{28,0},{1,29},{... | collective-permute-start | bytes 1640 | tf_op jit(solution)/shard_map/ppermute | solution.py:29
  82.5 1.1 %copy-start.5 = (f32[2,34,5136]{2,0,1:T(2,128)}, f32[2,34,5136]{2,0,1:T(2,128)S(1)}, u32[]{:S(2)}) copy-start(f32[2,34,5136]{2,0,1:T(2,128)S(1)} %get-tuple-element.40) | copy-start | bytes 4190980
